TPU v7x, 128 devices: a whole 4x4x4 slice. The times are simulated.
128 devices in a mesh: dp: 8 (over y_lo, x), zero: 16 (over z, y_hi, core).
Axes of the slice: x: 4, y: 4 (y_hi: 2, y_lo: 2; y = y_hi * 2 + y_lo), z: 4, core: 2. Of those that a mesh axis runs over, the one named last changes fastest.
Arguments:
- tokens: bfloat16 [16384, 1024], P(('dp', 'zero')), may hold values from -24 to 24
- cotangent: bfloat16 [16384, 1024], P(('dp', 'zero')), may hold values from -6 to 6
- segments: int32 [128, 128], P(('dp', 'zero')), may hold values from 0 to 3, never falling along the last dimension, each value on 1 to 64 neighbouring positions
- w_qkv: float32 [1024, 3072], P('zero'), may hold values from -0.1875 to 0.1875
- w_out: float32 [1024, 1024], P('zero'), may hold values from -0.75 to 0.75
- w_fc: float32 [1024, 4096], P('zero'), may hold values from -0.1875 to 0.1875
- w_proj: float32 [4096, 1024], P('zero'), may hold values from -0.09375 to 0.09375
- vectors: float32 [12, 1024], P(None, 'zero'), may hold values from -1.2 to 1.6, as said below
- mean_qkv: float32 [1024, 3072], P('zero'), may hold values from -0.6 to 0.6
- mean_out: float32 [1024, 1024], P('zero'), may hold values from -0.6 to 0.6
- mean_fc: float32 [1024, 4096], P('zero'), may hold values from -0.6 to 0.6
- mean_proj: float32 [4096, 1024], P('zero'), may hold values from -0.6 to 0.6
- mean_vectors: float32 [12, 1024], P(None, 'zero'), may hold values from -0.6 to 0.6
- square_qkv: float32 [1024, 3072], P('zero'), may hold values from 1e-05 to 0.001
- square_out: float32 [1024, 1024], P('zero'), may hold values from 1e-05 to 0.001
- square_fc: float32 [1024, 4096], P('zero'), may hold values from 1e-05 to 0.001
- square_proj: float32 [4096, 1024], P('zero'), may hold values from 1e-05 to 0.001
- square_vectors: float32 [12, 1024], P(None, 'zero'), may hold values from 1e-05 to 0.001
Outputs:
- block_out: bfloat16 [16384, 1024], P(('dp', 'zero'))
- input_grad: bfloat16 [16384, 1024], P(('dp', 'zero'))
- grad_qkv: float32 [1024, 3072], P('zero')
- grad_out: float32 [1024, 1024], P('zero')
- grad_fc: float32 [1024, 4096], P('zero')
- grad_proj: float32 [4096, 1024], P('zero')
- grad_vectors: float32 [12, 1024], P(None, 'zero')
- next_qkv: float32 [1024, 3072], P('zero')
- next_out: float32 [1024, 1024], P('zero')
- next_fc: float32 [1024, 4096], P('zero')
- next_proj: float32 [4096, 1024], P('zero')
- next_vectors: float32 [12, 1024], P(None, 'zero')
- next_mean_qkv: float32 [1024, 3072], P('zero')
- next_mean_out: float32 [1024, 1024], P('zero')
- next_mean_fc: float32 [1024, 4096], P('zero')
- next_mean_proj: float32 [4096, 1024], P('zero')
- next_mean_vectors: float32 [12, 1024], P(None, 'zero')
- next_square_qkv: float32 [1024, 3072], P('zero')
- next_square_out: float32 [1024, 1024], P('zero')
- next_square_fc: float32 [1024, 4096], P('zero')
- next_square_proj: float32 [4096, 1024], P('zero')
- next_square_vectors: float32 [12, 1024], P(None, 'zero')
Inputs may be any that keep to these rules, and one draw needn't show every extreme that they name: `segments`: in each row of 128 tokens the segment numbers never fall; each of the 4 documents of a row has 1 to 64 tokens, and one has exactly 64. `vectors`: rows 0 and 5 lie within 0.4 to 1.6; the other rows within -1.2 to 1.2.
All inputs are finite; a program needn't handle non-finite values.
Results may differ from a plain program's by a relative error of at most 0.04.
Values may be sent and summed in bfloat16 or wider, within the bound.
A program may use at most 192 MiB of HBM per device.

v0:
```python
from functools import partial
import jax
import jax.numpy as jnp
from jax import lax
from jax.sharding import PartitionSpec as P

HEADS = 16
SEQ = 128
ADAM_STEP = 3
eps_norm = 1e-05
beta_first = 0.9
beta_second = 0.999
eps_adam = 1e-08
rate_matrix = 0.02
rate_vector = 0.15
decay_matrix = 0.1


def sent_together(arrays, axis, dim, along):
    widths = [a.shape[along] for a in arrays]
    both = jnp.concatenate(arrays, axis=along)
    result = lax.all_gather(both, axis, axis=dim, tiled=True)
    return tuple(jnp.split(result, [sum(widths[:k]) for k in range(1, len(widths))], axis=along))


def in_one_piece(arrays, axis, dim, along):
    ends, at = ([], 0)
    for a in arrays[:-1]:
        at += a.shape[along]
        ends.append(at)
    both = jnp.concatenate(arrays, axis=along)
    return tuple(
        jnp.split(lax.psum_scatter(both, axis, scatter_dimension=dim, tiled=True), ends, axis=along)
    )


def gelu_tanh(inputs):
    inner = 0.7978845608028654 * (inputs + 0.044715 * inputs * inputs * inputs)
    return 0.5 * inputs * (1.0 + jnp.tanh(inner))


def layer_norm(inputs, gain_row, bias_row):
    average = jnp.mean(inputs, axis=-1, keepdims=True)
    centred = inputs - average
    variance = jnp.mean(centred * centred, axis=-1, keepdims=True)
    return centred * lax.rsqrt(variance + eps_norm) * gain_row + bias_row


def allowed_mask(seg_rows):
    length = seg_rows.shape[1]
    places = lax.iota(jnp.int32, length)
    causal = places[:, None] >= places[None, :]
    same_doc = seg_rows[:, :, None] == seg_rows[:, None, :]
    return jnp.logical_and(same_doc, causal[None])[:, None]


def attend_scores(queries, keys_in, seg_rows):
    scaling = queries.shape[-1] ** (-0.5)
    scores = (
        jnp.einsum("rqhe,rkhe->rhqk", queries, keys_in, preferred_element_type=jnp.float32)
        * scaling
    )
    return (scores, allowed_mask(seg_rows), scaling)


def attention_forward(queries, keys_in, values, seg_rows):
    scores, allowed, scaling = attend_scores(queries, keys_in, seg_rows)
    exponent = jnp.where(allowed, jnp.exp(scores), 0.0)
    log_total = jnp.log(jnp.sum(exponent, axis=-1, keepdims=True))
    attn_weights = jnp.where(allowed, jnp.exp(scores - log_total), 0.0).astype(jnp.bfloat16)
    attended = jnp.einsum(
        "rhqk,rkhe->rqhe", attn_weights, values, preferred_element_type=jnp.float32
    )
    return (attended.astype(jnp.bfloat16), log_total)


def attention_backward(queries, keys_in, values, seg_rows, log_total, grad_att):
    scores, allowed, scaling = attend_scores(queries, keys_in, seg_rows)
    weights_full = jnp.where(allowed, jnp.exp(scores - log_total), 0.0)
    weights_half = weights_full.astype(jnp.bfloat16)
    grad_values = jnp.einsum(
        "rhqk,rqhe->rkhe", weights_half, grad_att, preferred_element_type=jnp.float32
    )
    grad_weights = jnp.einsum(
        "rqhe,rkhe->rhqk", grad_att, values, preferred_element_type=jnp.float32
    )
    row_dot = jnp.sum(weights_full * grad_weights, axis=-1, keepdims=True)
    grad_scores = (weights_full * (grad_weights - row_dot) * scaling).astype(jnp.bfloat16)
    grad_queries = jnp.einsum(
        "rhqk,rkhe->rqhe", grad_scores, keys_in, preferred_element_type=jnp.float32
    )
    grad_keys = jnp.einsum(
        "rhqk,rqhe->rkhe", grad_scores, queries, preferred_element_type=jnp.float32
    )
    return (grad_queries, grad_keys, grad_values)


def block_pass(tokens_in, cot_in, seg_rows, qkv_mat, out_mat, fc_mat, proj_mat, vec_rows):
    count_tok = tokens_in.shape[0]
    width = tokens_in.shape[1]
    head_width = width // HEADS
    row_count = count_tok // SEQ
    split_shape = (row_count, SEQ, HEADS, head_width)
    tokens32 = tokens_in.astype(jnp.float32)
    normed_one = layer_norm(tokens32, vec_rows[0], vec_rows[1]).astype(jnp.bfloat16)
    projected = jnp.dot(normed_one, qkv_mat, preferred_element_type=jnp.float32)
    queries = (projected[:, :width] + vec_rows[2]).astype(jnp.bfloat16).reshape(split_shape)
    keys_in = projected[:, width : 2 * width].astype(jnp.bfloat16).reshape(split_shape)
    values = (projected[:, 2 * width :] + vec_rows[3]).astype(jnp.bfloat16).reshape(split_shape)
    attended, log_total = attention_forward(queries, keys_in, values, seg_rows)
    attended = attended.reshape(count_tok, width)
    middle = tokens32 + jnp.dot(attended, out_mat, preferred_element_type=jnp.float32) + vec_rows[4]
    normed_two = layer_norm(middle, vec_rows[5], vec_rows[6]).astype(jnp.bfloat16)
    fc_bias = vec_rows[8:].reshape(-1)
    hidden_pre = jnp.dot(normed_two, fc_mat, preferred_element_type=jnp.float32) + fc_bias
    hidden = gelu_tanh(hidden_pre).astype(jnp.bfloat16)
    block_out = (
        middle + jnp.dot(hidden, proj_mat, preferred_element_type=jnp.float32) + vec_rows[7]
    ).astype(jnp.bfloat16)
    cot32 = cot_in.astype(jnp.float32)
    grad_proj = jnp.dot(hidden.T, cot_in, preferred_element_type=jnp.float32)
    grad_hidden = jnp.dot(cot_in, proj_mat.T, preferred_element_type=jnp.float32)
    gelu_back = jax.vjp(gelu_tanh, hidden_pre)[1]
    grad_pre = gelu_back(grad_hidden)[0]
    grad_pre_half = grad_pre.astype(jnp.bfloat16)
    grad_fc = jnp.dot(normed_two.T, grad_pre_half, preferred_element_type=jnp.float32)
    grad_normed_two = jnp.dot(grad_pre_half, fc_mat.T, preferred_element_type=jnp.float32)
    norm_two_back = jax.vjp(layer_norm, middle, vec_rows[5], vec_rows[6])[1]
    grad_mid_norm, grad_gain_two, grad_bias_two = norm_two_back(grad_normed_two)
    grad_middle = cot32 + grad_mid_norm
    grad_middle_half = grad_middle.astype(jnp.bfloat16)
    grad_out = jnp.dot(attended.T, grad_middle_half, preferred_element_type=jnp.float32)
    grad_attended = jnp.dot(grad_middle_half, out_mat.T, preferred_element_type=jnp.float32)
    grad_attended = grad_attended.astype(jnp.bfloat16).reshape(split_shape)
    grad_queries, grad_keys, grad_values = attention_backward(
        queries, keys_in, values, seg_rows, log_total, grad_attended
    )
    flat_queries = grad_queries.reshape(count_tok, width)
    flat_keys = grad_keys.reshape(count_tok, width)
    flat_values = grad_values.reshape(count_tok, width)
    grad_projected = jnp.concatenate([flat_queries, flat_keys, flat_values], axis=1).astype(
        jnp.bfloat16
    )
    grad_qkv = jnp.dot(normed_one.T, grad_projected, preferred_element_type=jnp.float32)
    grad_normed_one = jnp.dot(grad_projected, qkv_mat.T, preferred_element_type=jnp.float32)
    norm_one_back = jax.vjp(layer_norm, tokens32, vec_rows[0], vec_rows[1])[1]
    grad_tok_norm, grad_gain_one, grad_bias_one = norm_one_back(grad_normed_one)
    input_grad = (grad_middle + grad_tok_norm).astype(jnp.bfloat16)
    small_rows = jnp.stack(
        [
            grad_gain_one,
            grad_bias_one,
            jnp.sum(flat_queries, axis=0),
            jnp.sum(flat_values, axis=0),
            jnp.sum(grad_middle, axis=0),
            grad_gain_two,
            grad_bias_two,
            jnp.sum(cot32, axis=0),
        ]
    )
    grad_vec = jnp.concatenate([small_rows, jnp.sum(grad_pre, axis=0).reshape(-1, width)], axis=0)
    return (block_out, input_grad, (grad_qkv, grad_out, grad_fc, grad_proj, grad_vec))


def adam_step(weight, gradient, mean_old, square_old, rate, decay):
    mean_new = beta_first * mean_old + (1.0 - beta_first) * gradient
    square_new = beta_second * square_old + (1.0 - beta_second) * gradient * gradient
    mean_hat = mean_new / (1.0 - beta_first**ADAM_STEP)
    square_hat = square_new / (1.0 - beta_second**ADAM_STEP)
    weight_new = weight - rate * (mean_hat / (jnp.sqrt(square_hat) + eps_adam) + decay * weight)
    return (weight_new, mean_new, square_new)


def local(
    tokens,
    cotangent,
    segments,
    w_qkv,
    w_out,
    w_fc,
    w_proj,
    vectors,
    mean_qkv,
    mean_out,
    mean_fc,
    mean_proj,
    mean_vectors,
    square_qkv,
    square_out,
    square_fc,
    square_proj,
    square_vectors,
):
    dp_size = lax.axis_size("dp")
    zero_size = lax.axis_size("zero")
    replicas = dp_size * zero_size
    qkv_mat, out_mat, fc_mat, proj_mat, vec_half = (
        *sent_together(
            (w_qkv.astype(jnp.bfloat16), w_out.astype(jnp.bfloat16), w_fc.astype(jnp.bfloat16)),
            "zero",
            0,
            1,
        ),
        lax.all_gather(w_proj.astype(jnp.bfloat16), "zero", axis=0, tiled=True),
        lax.all_gather(vectors.astype(jnp.bfloat16), "zero", axis=1, tiled=True),
    )
    vec_rows = vec_half.astype(jnp.float32)
    block_out, input_grad, local_grads = block_pass(
        tokens, cotangent, segments, qkv_mat, out_mat, fc_mat, proj_mat, vec_rows
    )
    pieces = (
        *tuple(
            (
                part.astype(jnp.float32)
                for part in in_one_piece(
                    (
                        local_grads[0].astype(jnp.bfloat16),
                        local_grads[1].astype(jnp.bfloat16),
                        local_grads[2].astype(jnp.bfloat16),
                    ),
                    "zero",
                    0,
                    1,
                )
            )
        ),
        lax.psum_scatter(
            local_grads[3].astype(jnp.bfloat16), "zero", scatter_dimension=0, tiled=True
        ).astype(jnp.float32),
        lax.psum_scatter(
            local_grads[4].astype(jnp.bfloat16), "zero", scatter_dimension=1, tiled=True
        ).astype(jnp.float32),
    )
    summed = (
        lax.psum(pieces[0].astype(jnp.bfloat16), "dp").astype(jnp.float32),
        lax.psum(pieces[1].astype(jnp.bfloat16), "dp").astype(jnp.float32),
        lax.psum(pieces[2].astype(jnp.bfloat16), "dp").astype(jnp.float32),
        lax.psum(pieces[3].astype(jnp.bfloat16), "dp").astype(jnp.float32),
        lax.psum(pieces[4].astype(jnp.bfloat16), "dp").astype(jnp.float32),
    )
    grads = jax.tree.map(partial(jnp.multiply, 1.0 / replicas), summed)
    first = adam_step(w_qkv, grads[0], mean_qkv, square_qkv, rate_matrix, decay_matrix)
    second = adam_step(w_out, grads[1], mean_out, square_out, rate_matrix, decay_matrix)
    third = adam_step(w_fc, grads[2], mean_fc, square_fc, rate_matrix, decay_matrix)
    fourth = adam_step(w_proj, grads[3], mean_proj, square_proj, rate_matrix, decay_matrix)
    fifth = adam_step(vectors, grads[4], mean_vectors, square_vectors, rate_vector, 0.0)
    return (
        block_out,
        input_grad,
        grads[0],
        grads[1],
        grads[2],
        grads[3],
        grads[4],
        first[0],
        second[0],
        third[0],
        fourth[0],
        fifth[0],
        first[1],
        second[1],
        third[1],
        fourth[1],
        fifth[1],
        first[2],
        second[2],
        third[2],
        fourth[2],
        fifth[2],
    )


def solution(mesh):
    placed = (
        P(("dp", "zero"), None),
        P(("dp", "zero"), None),
        P(("dp", "zero"), None),
        P("zero", None),
        P("zero", None),
        P("zero", None),
        P("zero", None),
        P(None, "zero"),
        P("zero", None),
        P("zero", None),
        P("zero", None),
        P("zero", None),
        P(None, "zero"),
        P("zero", None),
        P("zero", None),
        P("zero", None),
        P("zero", None),
        P(None, "zero"),
    )
    return jax.shard_map(
        local,
        mesh=mesh,
        in_specs=placed,
        out_specs=(
            P(("dp", "zero"), None),
            P(("dp", "zero"), None),
            P("zero", None),
            P("zero", None),
            P("zero", None),
            P("zero", None),
            P(None, "zero"),
            P("zero", None),
            P("zero", None),
            P("zero", None),
            P("zero", None),
            P(None, "zero"),
            P("zero", None),
            P("zero", None),
            P("zero", None),
            P("zero", None),
            P(None, "zero"),
            P("zero", None),
            P("zero", None),
            P("zero", None),
            P("zero", None),
            P(None, "zero"),
        ),
        check_vma=False,
    )
```

profile of v0, /device:TPU:0, one launch (start us, length us, event | category | flops | bytes accessed | tf_op | source)
XLA Modules:
  0.0 683.3 jit_solution(5639549732843436723)
XLA Ops:
  10.9 26.1 %all-gather = bf16[16,64,12]{1,2,0:T(8,128)(2,1)S(1)} all-gather(bf16[1,64,12]{1,2,0:T(8,128)(2,1)S(1)} %convert_bitcast_fusion), channel_id=1, replica_groups=mesh['dp'=8,'zero'=16] {'zero'}, dimensions={0}, use_global_device_ids=true | all-gather | bytes 26112 | tf_op jit(solution)/shard_map/all_gather | solution.py:205
  37.6 49.3 %all-gather.6.cloned.1.call-done = bf16[4096,1024]{1,0:T(8,128)(2,1)} async-done(((bf16[256,1024]{1,0:T(8,128)(2,1)}), bf16[4096,1024]{1,0:T(8,128)(2,1)}) %all-gather.6.cloned.1.call-update) | async-done | bytes 8388624 | tf_op jit(solution)/shard_map/all_gather | solution.py:204
  86.9 6.2 fusion.127
  93.2 103.9 %all-gather.4.cloned.1.call-done = bf16[1024,8192]{1,0:T(8,128)(2,1)} async-done(((bf16[64,8192]{1,0:T(8,128)(2,1)}), bf16[1024,8192]{1,0:T(8,128)(2,1)}) %all-gather.4.cloned.1.call-update) | async-done | bytes 16777232 | tf_op jit(solution)/shard_map/all_gather | solution.py:22
  197.1 3.9 fusion.8
  212.9 7.9 %fusion.118 = (bf16[4096]{0:T(1024)(128)(2,1)S(1)}, bf16[128,4096]{1,0:T(8,128)(2,1)S(1)}, f32[128,4096]{1,0:T(8,128)}) fusion(f32[128,4096]{1,0:T(8,128)S(1)} %fusion.127, f32[4096]{0:T(1024)S(1)} %bitcast.99, bf16[1024,8192]{1,0:T(8,128)(2,1)} %all-gather.4.cloned.1.call-done, f32[128,1024]{1,0:T(8,128)S(1)} %get-tuple-element.74, ...), kind=kOutput, calls=%fused_computation.155 | convolution fusion | flops 1088024576 | bytes 14189568 | tf_op jit(solution)/shard_map/dot_general | solution.py:115
  220.9 6.8 multiply_reduce_fusion.1
  231.5 3.0 fusion.121
  236.8 2.8 convolution_convert_fusion.4
  239.6 3.4 fusion.122
  243.0 3.2 convolution_convert_fusion.3
  246.1 5.7 convolution_convert_fusion.1
  251.8 2.9 copy.82
  254.7 3.2 convolution_convert_fusion.2
  258.3 6.6 pad_maximum_fusion
  266.5 6.2 convolution_convert_fusion
  273.0 6.6 fusion.107
  282.3 127.4 %reduce-scatter.6.cloned.1.call-done = bf16[64,8192]{1,0:T(8,128)(2,1)} async-done(((bf16[1024,8192]{1,0:T(8,128)(2,1)}), bf16[64,8192]{1,0:T(8,128)(2,1)}) %reduce-scatter.6.cloned.1.call-update) | async-done | bytes 1048592 | tf_op jit(solution)/shard_map/reduce_scatter | solution.py:33
  414.9 99.2 %reduce-scatter.8.cloned.1.call-done = bf16[256,1024]{1,0:T(8,128)(2,1)} async-done(((bf16[4096,1024]{1,0:T(8,128)(2,1)}), bf16[256,1024]{1,0:T(8,128)(2,1)}) %reduce-scatter.8.cloned.1.call-update) | async-done | bytes 524304 | tf_op jit(solution)/shard_map/reduce_scatter | solution.py:227
  514.1 5.6 fusion.39
  519.7 62.4 %reduce-scatter.10.cloned.1.call-done = bf16[64,12]{1,0:T(8,128)(2,1)} async-done(((bf16[1024,12]{1,0:T(8,128)(2,1)}), bf16[64,12]{1,0:T(8,128)(2,1)}) %reduce-scatter.10.cloned.1.call-update) | async-done | bytes 1552
  582.8 19.0 %psum.39 = bf16[12,64]{1,0:T(8,128)(2,1)S(1)} all-reduce(bf16[12,64]{1,0:T(8,128)(2,1)S(1)} %copy.88), channel_id=1, replica_groups=mesh['dp'=8,'zero'=16] {'dp'}, use_global_device_ids=true, to_apply=%region_26.27 | all-reduce | flops 768 | bytes 3072 | tf_op jit(solution)/shard_map/psum | solution.py:239
  602.5 62.1 %all-reduce.3.cloned.1.call-done = (bf16[64,3072]{1,0:T(8,128)(2,1)}, bf16[64,1024]{1,0:T(8,128)(2,1)}, bf16[64,4096]{1,0:T(8,128)(2,1)}, bf16[256,1024]{1,0:T(8,128)(2,1)}) async-done(((bf16[64,3072]{1,0:T(8,128)(2,1)}, bf16[64,1024]{1,0:T(8,128)(2,1)}, bf16[64,4096]{1,0:T(8,128)(2,1)}, bf16[256,1024]{1,0:T(8,128)(2,1)}), (bf16[64,3072]{1,0:T(8,128)(2,1)}, bf16[64,1024]{1,0:T(8,128)(2,1)}, ...) | async-done | bytes 1572880 | tf_op jit(solution)/shard_map/psum | solution.py:235
  666.9 3.4 multiply_subtract_fusion.2
  (136 shorter events, 42.1 us)
Async XLA Ops:
  7.2 79.7 %all-gather.6.cloned.1.call-start = ((), (), s32[]{:S(2)}) async-start(), calls=%async_computation.4 | async-start | bytes 8912896 | tf_op jit(solution)/shard_map/all_gather | solution.py:204
  9.5 187.5 %all-gather.4.cloned.1.call-start = ((), (), s32[]{:S(2)}) async-start(), calls=%async_computation.3 | async-start | bytes 17825792 | tf_op jit(solution)/shard_map/all_gather | solution.py:22
  9.8 27.4 %copy-start.1 = (bf16[128,1024]{1,0:T(8,128)(2,1)S(1)}, bf16[128,1024]{1,0:T(8,128)(2,1)}, u32[]{:S(2)}) copy-start(bf16[128,1024]{1,0:T(8,128)(2,1)} %param.18) | copy-start | bytes 786436
  9.8 27.7 %copy-start.32 = (s32[1,128]{1,0:T(1,128)S(1)}, s32[1,128]{1,0:T(1,128)}, u32[]{:S(2)}) copy-start(s32[1,128]{1,0:T(1,128)} %param.20) | copy-start | bytes 1540
  9.8 77.2 %copy-start.2 = (bf16[128,1024]{1,0:T(8,128)(2,1)S(1)}, bf16[128,1024]{1,0:T(8,128)(2,1)}, u32[]{:S(2)}) copy-start(bf16[128,1024]{1,0:T(8,128)(2,1)} %param.19) | copy-start | bytes 786436
  10.9 398.8 %reduce-scatter.6.cloned.1.call-start = ((), (), s32[]{:S(2)}) async-start(), calls=%async_computation.5 | async-start | bytes 17825792 | tf_op jit(solution)/shard_map/reduce_scatter | solution.py:33
  202.8 4.9 copy-start.20
  204.0 6.4 copy-start.23
  220.9 6.8 copy-start.15
  227.9 15.0 %copy-start.4 = (f32[128,1024]{1,0:T(8,128)}, f32[128,1024]{1,0:T(8,128)S(1)}, u32[]{:S(2)}) copy-start(f32[128,1024]{1,0:T(8,128)S(1)} %get-tuple-element.56) | copy-start | bytes 1572868
  230.6 6.2 copy-start.22
  231.5 8.1 %copy-start.21 = (bf16[128,1024]{0,1:T(8,128)(2,1)S(1)}, bf16[128,1024]{0,1:T(8,128)(2,1)}, u32[]{:S(2)}) copy-start(bf16[128,1024]{0,1:T(8,128)(2,1)} %copy-done.20) | copy-start | bytes 786436
  239.6 6.5 copy-start.16
  254.7 3.6 copy-start
  264.9 249.1 %reduce-scatter.8.cloned.1.call-start = ((), (), s32[]{:S(2)}) async-start(), calls=%async_computation.6 | async-start | bytes 8912896 | tf_op jit(solution)/shard_map/reduce_scatter | solution.py:227
  272.7 309.3 %reduce-scatter.10.cloned.1.call-start = ((), (), s32[]{:S(2)}) async-start(), calls=%async_computation.7 | async-start | bytes 278528
  273.0 6.9 %copy-start.5 = (f32[128,1024]{1,0:T(8,128)S(1)}, f32[128,1024]{1,0:T(8,128)}, u32[]{:S(2)}) copy-start(f32[128,1024]{1,0:T(8,128)} %copy-done.4) | copy-start | bytes 1572868
  282.0 382.6 %all-reduce.3.cloned.1.call-start = ((), (), s32[]{:S(2)}) async-start(), calls=%async_computation.8 | async-start | bytes 3145728 | tf_op jit(solution)/shard_map/psum | solution.py:235
  514.0 87.8 %copy-start.30 = (f32[12,64]{1,0:T(8,128)S(1)}, f32[12,64]{1,0:T(8,128)}, u32[]{:S(2)}) copy-start(f32[12,64]{1,0:T(8,128)} %param.30) | copy-start | bytes 9220
  514.0 87.8 %copy-start.31 = (f32[12,64]{1,0:T(8,128)S(1)}, f32[12,64]{1,0:T(8,128)}, u32[]{:S(2)}) copy-start(f32[12,64]{1,0:T(8,128)} %param.35) | copy-start | bytes 9220
  519.7 147.2 %copy-start.10 = (f32[64,3072]{1,0:T(8,128)S(1)}, f32[64,3072]{1,0:T(8,128)}, u32[]{:S(2)}) copy-start(f32[64,3072]{1,0:T(8,128)} %param.21) | copy-start | bytes 2359300
  519.7 147.2 %copy-start.25 = (f32[64,3072]{1,0:T(8,128)S(1)}, f32[64,3072]{1,0:T(8,128)}, u32[]{:S(2)}) copy-start(f32[64,3072]{1,0:T(8,128)} %param.26) | copy-start | bytes 2359300
  666.9 3.5 copy-start.7
  666.9 3.4 copy-start.11
  (15 other events, 33.6 us)
Sparse Core Ops, SparseCore 0:
  11.1 75.7 all-gather.5
  90.0 107.0 all-gather.3
  265.0 144.5 reduce-scatter.5
  413.8 100.1 reduce-scatter.7
  518.1 63.8 reduce-scatter.9
  585.8 78.7 all-reduce.2
where the time goes:
time: 684 us; the launch traced here: 683 us
  waiting for transfers between devices  504 us (74%)
  matrix products  74.7 us (11%)
  blocking collectives  45.1 us (7%)
  other arithmetic  26.1 us (4%)
  local copies, waits for them, and re-layouts  18 us (3%)
  between operations  14.6 us (2%)
    reduce_scatter x1, waiting for transfers between devices, in_one_piece(): lax.psum_scatter(both, axis, scatter_dimension=dim, tiled=True)  127 us
    all_gather x1, waiting for transfers between devices, sent_together(): result = lax.all_gather(both, axis, axis=dim, tiled=True)  104 us
    reduce_scatter x1, waiting for transfers between devices, local(): lax.psum_scatter(local_grads[3].astype(jnp.bfloat16), 'zero', scatter_dim...  99.2 us
    unnamed x7, waiting for transfers between devices  62.5 us
    psum x1, waiting for transfers between devices, local(): lax.psum(pieces[0].astype(jnp.bfloat16), 'dp').astype(jnp.float32)  62.1 us
    all_gather x1, waiting for transfers between devices, local(): lax.all_gather(w_proj.astype(jnp.bfloat16), 'zero', axis=0, tiled=True)  49.3 us
    all_gather x1, blocking collectives, local(): lax.all_gather(vectors.astype(jnp.bfloat16), 'zero', axis=1, tiled=True)  26.1 us
    psum x1, blocking collectives, local(): lax.psum(pieces[4].astype(jnp.bfloat16), 'dp').astype(jnp.float32)  19 us
  transfers between devices with their start and end apart: 6, of which 6 were waited for; matrix products, arithmetic and copies ran while one was open for 5% of the time, Pallas kernels for 0%

commit v1 on v0

--- a/solution.py
+++ b/solution.py
@@ -14,6 +14,11 @@
 rate_matrix = 0.02
 rate_vector = 0.15
 decay_matrix = 0.1
+
+
+def gather_and_add(x, axis):
+    pieces = lax.all_gather(x, axis)
+    return jnp.sum(pieces, axis=0)
 
 
 def sent_together(arrays, axis, dim, along):
@@ -232,7 +237,7 @@
         ).astype(jnp.float32),
     )
     summed = (
-        lax.psum(pieces[0].astype(jnp.bfloat16), "dp").astype(jnp.float32),
+        gather_and_add(pieces[0].astype(jnp.bfloat16), "dp").astype(jnp.float32),
         lax.psum(pieces[1].astype(jnp.bfloat16), "dp").astype(jnp.float32),
         lax.psum(pieces[2].astype(jnp.bfloat16), "dp").astype(jnp.float32),
         lax.psum(pieces[3].astype(jnp.bfloat16), "dp").astype(jnp.float32),

time: 684 us -> 721 us (1.054)
  waiting for transfers between devices: 504 us -> 539 us
    all_gather x0 -> x1, waiting for transfers between devices: none -> 36.7 us  [gather_and_add(): pieces = lax.all_gather(x, axis)]
    unnamed x7 -> x8, waiting for transfers between devices: 62.5 us -> 60.4 us
  transfers between devices with their start and end apart: 6 -> 7, of which waited for: 6 -> 7; matrix products, arithmetic and copies ran while one was open for 5% -> 6% of each run, Pallas kernels for 0% -> 0%
where the time goes in v1:
time: 721 us; the launch traced here: 720 us
  waiting for transfers between devices  539 us (75%)
  matrix products  74.7 us (10%)
  blocking collectives  45.1 us (6%)
  other arithmetic  28.9 us (4%)
  local copies, waits for them, and re-layouts  17.2 us (2%)
  between operations  14.7 us (2%)
    reduce_scatter x1, waiting for transfers between devices, in_one_piece(): lax.psum_scatter(both, axis, scatter_dimension=dim, tiled=True)  128 us
    all_gather x1, waiting for transfers between devices, sent_together(): result = lax.all_gather(both, axis, axis=dim, tiled=True)  104 us
    reduce_scatter x1, waiting for transfers between devices, local(): lax.psum_scatter(local_grads[3].astype(jnp.bfloat16), 'zero', scatter_dim...  101 us
    unnamed x8, waiting for transfers between devices  60.4 us
    psum x1, waiting for transfers between devices, local(): lax.psum(pieces[1].astype(jnp.bfloat16), 'dp').astype(jnp.float32)  60.1 us
    all_gather x1, waiting for transfers between devices, local(): lax.all_gather(w_proj.astype(jnp.bfloat16), 'zero', axis=0, tiled=True)  49.3 us
    all_gather x1, waiting for transfers between devices, gather_and_add(): pieces = lax.all_gather(x, axis)  36.7 us
    all_gather x1, blocking collectives, local(): lax.all_gather(vectors.astype(jnp.bfloat16), 'zero', axis=1, tiled=True)  26.1 us
  transfers between devices with their start and end apart: 7, of which 7 were waited for; matrix products, arithmetic and copies ran while one was open for 6% of the time, Pallas kernels for 0%

profile of v1, /device:TPU:0, one launch (start us, length us, event | category | flops | bytes accessed | tf_op | source)
XLA Modules:
  0.0 720.0 jit_solution(3183698781178678207)
XLA Ops:
  10.9 26.1 %all-gather.1 = bf16[16,64,12]{1,2,0:T(8,128)(2,1)S(1)} all-gather(bf16[1,64,12]{1,2,0:T(8,128)(2,1)S(1)} %convert_bitcast_fusion), channel_id=1, replica_groups=mesh['dp'=8,'zero'=16] {'zero'}, dimensions={0}, use_global_device_ids=true | all-gather | bytes 26112 | tf_op jit(solution)/shard_map/all_gather | solution.py:210
  37.6 49.3 %all-gather.8.cloned.1.call-done = bf16[4096,1024]{1,0:T(8,128)(2,1)} async-done(((bf16[256,1024]{1,0:T(8,128)(2,1)}), bf16[4096,1024]{1,0:T(8,128)(2,1)}) %all-gather.8.cloned.1.call-update) | async-done | bytes 8388624 | tf_op jit(solution)/shard_map/all_gather | solution.py:209
  86.9 6.2 fusion.127
  93.2 103.9 %all-gather.6.cloned.1.call-done = bf16[1024,8192]{1,0:T(8,128)(2,1)} async-done(((bf16[64,8192]{1,0:T(8,128)(2,1)}), bf16[1024,8192]{1,0:T(8,128)(2,1)}) %all-gather.6.cloned.1.call-update) | async-done | bytes 16777232 | tf_op jit(solution)/shard_map/all_gather | solution.py:27
  197.1 3.9 fusion.8
  212.9 7.9 %fusion.118 = (bf16[4096]{0:T(1024)(128)(2,1)S(1)}, bf16[128,4096]{1,0:T(8,128)(2,1)S(1)}, f32[128,4096]{1,0:T(8,128)}) fusion(f32[128,4096]{1,0:T(8,128)S(1)} %fusion.127, f32[4096]{0:T(1024)S(1)} %bitcast.101, bf16[1024,8192]{1,0:T(8,128)(2,1)} %all-gather.6.cloned.1.call-done, f32[128,1024]{1,0:T(8,128)S(1)} %get-tuple-element.73, ...), kind=kOutput, calls=%fused_computation.155 | convolution fusion | flops 1088024576 | bytes 14189568 | tf_op jit(solution)/shard_map/dot_general | solution.py:120
  220.9 6.8 multiply_reduce_fusion.1
  231.5 3.0 fusion.121
  239.6 3.4 fusion.122
  243.0 3.2 convolution_convert_fusion.3
  246.1 5.7 convolution_convert_fusion.1
  251.8 2.9 copy.82
  254.7 3.2 convolution_convert_fusion.2
  258.3 6.6 pad_maximum_fusion
  266.5 6.2 convolution_convert_fusion
  273.0 6.6 fusion.107
  282.0 127.6 %reduce-scatter.6.cloned.1.call-done = bf16[64,8192]{1,0:T(8,128)(2,1)} async-done(((bf16[1024,8192]{1,0:T(8,128)(2,1)}), bf16[64,8192]{1,0:T(8,128)(2,1)}) %reduce-scatter.6.cloned.1.call-update) | async-done | bytes 1048592 | tf_op jit(solution)/shard_map/reduce_scatter | solution.py:38
  413.1 101.0 %reduce-scatter.8.cloned.1.call-done = bf16[256,1024]{1,0:T(8,128)(2,1)} async-done(((bf16[4096,1024]{1,0:T(8,128)(2,1)}), bf16[256,1024]{1,0:T(8,128)(2,1)}) %reduce-scatter.8.cloned.1.call-update) | async-done | bytes 524304 | tf_op jit(solution)/shard_map/reduce_scatter | solution.py:232
  516.1 5.6 fusion.39
  521.8 60.3 %reduce-scatter.10.cloned.1.call-done = bf16[64,12]{1,0:T(8,128)(2,1)} async-done(((bf16[1024,12]{1,0:T(8,128)(2,1)}), bf16[64,12]{1,0:T(8,128)(2,1)}) %reduce-scatter.10.cloned.1.call-update) | async-done | bytes 1552
  582.8 19.0 %psum.31 = bf16[12,64]{1,0:T(8,128)(2,1)S(1)} all-reduce(bf16[12,64]{1,0:T(8,128)(2,1)S(1)} %copy.88), channel_id=1, replica_groups=mesh['dp'=8,'zero'=16] {'dp'}, use_global_device_ids=true, to_apply=%region_26.27 | all-reduce | flops 768 | bytes 3072 | tf_op jit(solution)/shard_map/psum | solution.py:244
  602.5 60.1 %all-reduce.3.cloned.1.call-done = (bf16[64,1024]{1,0:T(8,128)(2,1)}, bf16[64,4096]{1,0:T(8,128)(2,1)}, bf16[256,1024]{1,0:T(8,128)(2,1)}) async-done(((bf16[64,1024]{1,0:T(8,128)(2,1)}, bf16[64,4096]{1,0:T(8,128)(2,1)}, bf16[256,1024]{1,0:T(8,128)(2,1)}), (bf16[64,1024]{1,0:T(8,128)(2,1)}, bf16[64,4096]{1,0:T(8,128)(2,1)}, bf16[256,1024]{1,0:T(8,128)(2,1)})) %all-reduce.3.cloned.1.call-update) | async-done | bytes 1179664 | tf_op jit(solution)/shard_map/psum | solution.py:241
  664.9 4.4 multiply_subtract_fusion
  671.9 36.7 %all-gather.10.cloned.1.call-done = bf16[512,3072]{1,0:T(8,128)(2,1)} async-done(((bf16[64,3072]{1,0:T(8,128)(2,1)}), bf16[512,3072]{1,0:T(8,128)(2,1)}) %all-gather.10.cloned.1.call-update) | async-done | bytes 3145744 | tf_op jit(solution)/shard_map/all_gather | solution.py:20
  (136 shorter events, 46.1 us)
Async XLA Ops:
  7.2 79.7 %all-gather.8.cloned.1.call-start = ((), (), s32[]{:S(2)}) async-start(), calls=%async_computation.4 | async-start | bytes 8912896 | tf_op jit(solution)/shard_map/all_gather | solution.py:209
  9.5 187.5 %all-gather.6.cloned.1.call-start = ((), (), s32[]{:S(2)}) async-start(), calls=%async_computation.3 | async-start | bytes 17825792 | tf_op jit(solution)/shard_map/all_gather | solution.py:27
  9.8 27.4 %copy-start.1 = (bf16[128,1024]{1,0:T(8,128)(2,1)S(1)}, bf16[128,1024]{1,0:T(8,128)(2,1)}, u32[]{:S(2)}) copy-start(bf16[128,1024]{1,0:T(8,128)(2,1)} %param.18) | copy-start | bytes 786436
  9.8 27.7 %copy-start.30 = (s32[1,128]{1,0:T(1,128)S(1)}, s32[1,128]{1,0:T(1,128)}, u32[]{:S(2)}) copy-start(s32[1,128]{1,0:T(1,128)} %param.20) | copy-start | bytes 1540
  9.8 77.2 %copy-start.2 = (bf16[128,1024]{1,0:T(8,128)(2,1)S(1)}, bf16[128,1024]{1,0:T(8,128)(2,1)}, u32[]{:S(2)}) copy-start(bf16[128,1024]{1,0:T(8,128)(2,1)} %param.19) | copy-start | bytes 786436
  10.9 398.8 %reduce-scatter.6.cloned.1.call-start = ((), (), s32[]{:S(2)}) async-start(), calls=%async_computation.5 | async-start | bytes 17825792 | tf_op jit(solution)/shard_map/reduce_scatter | solution.py:38
  202.8 4.9 copy-start.18
  204.0 6.4 copy-start.21
  220.9 6.8 copy-start.13
  227.9 15.0 %copy-start.4 = (f32[128,1024]{1,0:T(8,128)}, f32[128,1024]{1,0:T(8,128)S(1)}, u32[]{:S(2)}) copy-start(f32[128,1024]{1,0:T(8,128)S(1)} %get-tuple-element.55) | copy-start | bytes 1572868
  230.6 6.2 copy-start.20
  231.5 8.1 %copy-start.19 = (bf16[128,1024]{0,1:T(8,128)(2,1)S(1)}, bf16[128,1024]{0,1:T(8,128)(2,1)}, u32[]{:S(2)}) copy-start(bf16[128,1024]{0,1:T(8,128)(2,1)} %copy-done.18) | copy-start | bytes 786436
  239.6 6.5 copy-start.14
  264.9 249.1 %reduce-scatter.8.cloned.1.call-start = ((), (), s32[]{:S(2)}) async-start(), calls=%async_computation.6 | async-start | bytes 8912896 | tf_op jit(solution)/shard_map/reduce_scatter | solution.py:232
  272.7 309.4 %reduce-scatter.10.cloned.1.call-start = ((), (), s32[]{:S(2)}) async-start(), calls=%async_computation.8 | async-start | bytes 278528
  273.0 6.9 copy-start.5
  282.0 380.6 %all-reduce.3.cloned.1.call-start = ((), (), s32[]{:S(2)}) async-start(), calls=%async_computation.9 | async-start | bytes 2359296 | tf_op jit(solution)/shard_map/psum | solution.py:241
  514.1 194.5 %all-gather.10.cloned.1.call-start = ((), (), s32[]{:S(2)}) async-start(), calls=%async_computation.7 | async-start | bytes 3538944 | tf_op jit(solution)/shard_map/all_gather | solution.py:20
  516.1 85.7 %copy-start.28 = (f32[12,64]{1,0:T(8,128)S(1)}, f32[12,64]{1,0:T(8,128)}, u32[]{:S(2)}) copy-start(f32[12,64]{1,0:T(8,128)} %param.30) | copy-start | bytes 9220
  516.1 85.7 %copy-start.29 = (f32[12,64]{1,0:T(8,128)S(1)}, f32[12,64]{1,0:T(8,128)}, u32[]{:S(2)}) copy-start(f32[12,64]{1,0:T(8,128)} %param.35) | copy-start | bytes 9220
  521.8 143.0 %copy-start.6 = (f32[256,1024]{1,0:T(8,128)S(1)}, f32[256,1024]{1,0:T(8,128)}, u32[]{:S(2)}) copy-start(f32[256,1024]{1,0:T(8,128)} %param.24) | copy-start | bytes 3145732
  671.9 39.1 %copy-start.10 = (f32[64,3072]{1,0:T(8,128)S(1)}, f32[64,3072]{1,0:T(8,128)}, u32[]{:S(2)}) copy-start(f32[64,3072]{1,0:T(8,128)} %param.21) | copy-start | bytes 2359300
  671.9 39.1 %copy-start.23 = (f32[64,3072]{1,0:T(8,128)S(1)}, f32[64,3072]{1,0:T(8,128)}, u32[]{:S(2)}) copy-start(f32[64,3072]{1,0:T(8,128)} %param.26) | copy-start | bytes 2359300
  671.9 39.1 %copy-start.24 = (f32[64,3072]{1,0:T(8,128)S(1)}, f32[64,3072]{1,0:T(8,128)}, u32[]{:S(2)}) copy-start(f32[64,3072]{1,0:T(8,128)} %param.31) | copy-start | bytes 2359300
  (14 other events, 36.2 us)
Sparse Core Ops, SparseCore 0:
  11.1 75.7 all-gather.7
  90.0 107.0 all-gather.5
  265.0 144.5 reduce-scatter.5
  413.8 100.2 reduce-scatter.7
  518.1 63.8 reduce-scatter.9
  585.8 76.7 all-reduce.2
  664.8 43.7 all-gather.9
